TPU v7x, 32 devices: a whole 2x2x4 slice. The times are simulated.
32 devices in a mesh: dp: 8 (over z, x), fsdp: 4 (over y, core).
Axes of the slice: x: 2, y: 2, z: 4, core: 2. Of those that a mesh axis runs over, the one named last changes fastest.
Arguments:
- tokens: bfloat16 [2, 8, 1024, 768], P(None, None, ('dp', 'fsdp')), may hold values from -6 to 6
- lengths: int32 [2, 8], replicated, may hold values from 1 to 1024, 5120 in all within a row
- deal: int32 [2, 8], replicated, may hold values from 0 to 7, each once within a row
- w_qkv: bfloat16 [1769472], P(('dp', 'fsdp')), may hold values from -0.21875 to 0.21875
- b_qkv: bfloat16 [2304], P(('dp', 'fsdp')), may hold values from -2 to 2
- w_out: bfloat16 [589824], P(('dp', 'fsdp')), may hold values from -3.5 to 3.5
- b_out: bfloat16 [768], P(('dp', 'fsdp')), may hold values from -2 to 2
- norm1_gain: bfloat16 [768], P(('dp', 'fsdp')), may hold values from 0.5 to 1.5
- norm1_bias: bfloat16 [768], P(('dp', 'fsdp')), may hold values from -2 to 2
- w_up: bfloat16 [2359296], P(('dp', 'fsdp')), may hold values from -0.21875 to 0.21875
- b_up: bfloat16 [3072], P(('dp', 'fsdp')), may hold values from -2 to 2
- w_down: bfloat16 [2359296], P(('dp', 'fsdp')), may hold values from -0.109375 to 0.109375
- b_down: bfloat16 [768], P(('dp', 'fsdp')), may hold values from -2 to 2
- norm2_gain: bfloat16 [768], P(('dp', 'fsdp')), may hold values from 0.5 to 1.5
- norm2_bias: bfloat16 [768], P(('dp', 'fsdp')), may hold values from -2 to 2
- cotangent: bfloat16 [2, 8, 1024, 768], P(None, None, ('dp', 'fsdp')), may hold values from -6 to 6
Outputs:
- output: bfloat16 [2, 8, 1024, 768], P(None, None, ('dp', 'fsdp'))
- tokens_grad: bfloat16 [2, 8, 1024, 768], P(None, None, ('dp', 'fsdp'))
- w_qkv_grad: float32 [1769472], P(('dp', 'fsdp'))
- b_qkv_grad: float32 [2304], P(('dp', 'fsdp'))
- w_out_grad: float32 [589824], P(('dp', 'fsdp'))
- b_out_grad: float32 [768], P(('dp', 'fsdp'))
- norm1_gain_grad: float32 [768], P(('dp', 'fsdp'))
- norm1_bias_grad: float32 [768], P(('dp', 'fsdp'))
- w_up_grad: float32 [2359296], P(('dp', 'fsdp'))
- b_up_grad: float32 [3072], P(('dp', 'fsdp'))
- w_down_grad: float32 [2359296], P(('dp', 'fsdp'))
- b_down_grad: float32 [768], P(('dp', 'fsdp'))
- norm2_gain_grad: float32 [768], P(('dp', 'fsdp'))
- norm2_bias_grad: float32 [768], P(('dp', 'fsdp'))
Inputs may be any that keep to these rules, and one draw needn't show every extreme that they name: In each micro-batch the lengths sum to 5120 and the largest is 1024. Each row of deal is a permutation of the slots of its micro-batch.
All inputs are finite; a program needn't handle non-finite values.
Results may differ from a plain program's by a relative error of at most 0.017.
Values may be sent and summed in bfloat16 or wider, within the bound.
No kernel may reach another device: no remote copies, remote signals or barrier semaphores. Data moves between devices by JAX's collectives and lax.ppermute only.
A program may use at most 256 MiB of HBM per device.

v0:
```python
import math

import jax
import jax.numpy as jnp
from jax import lax
from jax.sharding import PartitionSpec as P

D = 768
HEADS = 12
HD = 64
FF = 3072


def rotate(values_in, places, backward):
    half_dim = HD // 2
    frequency = 10000.0 ** (-(2.0 * jnp.arange(half_dim, dtype=jnp.float32)) / HD)
    angles = places.astype(jnp.float32)[:, None] * frequency[None, :]
    cosine = jnp.cos(angles)[:, None, :]
    sine_part = jnp.sin(angles)[:, None, :]
    if backward:
        sine_part = -sine_part
    shaped = values_in.reshape(values_in.shape[:-1] + (HEADS, half_dim, 2))
    even_part = shaped[..., 0]
    odd_part = shaped[..., 1]
    turned = jnp.stack(
        [even_part * cosine - odd_part * sine_part, even_part * sine_part + odd_part * cosine],
        axis=-1,
    )
    return turned.reshape(values_in.shape)


def normalize(row_data, norm_gain, offset):
    average = jnp.mean(row_data, axis=-1, keepdims=True)
    centered = row_data - average
    variance = jnp.mean(centered * centered, axis=-1, keepdims=True)
    inverse = lax.rsqrt(variance + 1e-05)
    standard = centered * inverse
    return (standard * norm_gain + offset, standard, inverse)


def normalize_back(grad_out, standard, inverse, norm_gain):
    grad_std = grad_out * norm_gain
    mean_grad = jnp.mean(grad_std, axis=-1, keepdims=True)
    mean_proj = jnp.mean(grad_std * standard, axis=-1, keepdims=True)
    grad_in = inverse * (grad_std - mean_grad - standard * mean_proj)
    return (grad_in, jnp.sum(grad_out * standard, axis=0), jnp.sum(grad_out, axis=0))


def gelu_slope(hidden):
    cumulative = 0.5 * (1.0 + lax.erf(hidden * (1.0 / math.sqrt(2.0))))
    return cumulative + hidden * jnp.exp(-0.5 * hidden * hidden) * (1.0 / math.sqrt(2.0 * math.pi))


def contract_rows(left, right):
    return lax.dot_general(
        left, right, (((0,), (0,)), ((), ())), preferred_element_type=jnp.float32
    )


def times_transposed(left, right):
    return lax.dot_general(
        left, right, (((1,), (1,)), ((), ())), preferred_element_type=jnp.float32
    )


def unpack(fetched):
    (
        qkv_flat,
        qkv_bias,
        out_flat,
        out_bias,
        gain_one,
        bias_one,
        up_flat,
        up_bias,
        down_flat,
        down_bias,
        gain_two,
        bias_two,
    ) = fetched
    as_float = jnp.float32
    return (
        qkv_flat.reshape(D, 3 * D),
        qkv_bias.astype(as_float),
        out_flat.reshape(D, D),
        out_bias.astype(as_float),
        gain_one.astype(as_float),
        bias_one.astype(as_float),
        up_flat.reshape(D, FF),
        up_bias.astype(as_float),
        down_flat.reshape(FF, D),
        down_bias.astype(as_float),
        gain_two.astype(as_float),
        bias_two.astype(as_float),
    )


def body(
    tokens,
    lengths,
    deal,
    w_qkv,
    b_qkv,
    w_out,
    b_out,
    norm1_gain,
    norm1_bias,
    w_up,
    b_up,
    w_down,
    b_down,
    norm2_gain,
    norm2_bias,
    cotangent,
):
    shards = (
        w_qkv,
        b_qkv,
        w_out,
        b_out,
        norm1_gain,
        norm1_bias,
        w_up,
        b_up,
        w_down,
        b_down,
        norm2_gain,
        norm2_bias,
    )
    n_dp = lax.axis_size("dp")
    n_fsdp = lax.axis_size("fsdp")
    dp_place = lax.axis_index("dp")
    fsdp_place = lax.axis_index("fsdp")
    batches, slot_count, home_rows, width = tokens.shape
    seq_dp = slot_count // n_dp
    local_rows = home_rows * n_dp
    full_len = local_rows * n_fsdp
    row_total = seq_dp * local_rows
    scale = 1.0 / math.sqrt(HD)
    dealt = jnp.stack([tokens[micro_idx][deal[micro_idx]] for micro_idx in range(batches)])
    dealt_grad = jnp.stack([cotangent[micro_idx][deal[micro_idx]] for micro_idx in range(batches)])
    work_in, work_grad = (
        lax.all_to_all(dealt, "dp", split_axis=1, concat_axis=2, tiled=True),
        lax.all_to_all(dealt_grad, "dp", split_axis=1, concat_axis=2, tiled=True),
    )
    row_ids = jnp.arange(local_rows, dtype=jnp.int32)
    query_places = (
        row_ids // home_rows * (n_fsdp * home_rows) + fsdp_place * home_rows + row_ids % home_rows
    )
    key_ids = jnp.arange(full_len, dtype=jnp.int32)
    owners = key_ids // local_rows
    within = key_ids % local_rows
    key_places = (
        within // home_rows * (n_fsdp * home_rows) + owners * home_rows + within % home_rows
    )
    outputs_list = []
    grads_list = []
    accumulated = ()
    owned = ()
    for micro_idx in range(batches):
        fetched = (
            lax.all_gather(shards[0], ("dp", "fsdp"), axis=0, tiled=True),
            lax.all_gather(shards[1], ("dp", "fsdp"), axis=0, tiled=True),
            lax.all_gather(shards[2], ("dp", "fsdp"), axis=0, tiled=True),
            lax.all_gather(shards[3], ("dp", "fsdp"), axis=0, tiled=True),
            lax.all_gather(shards[4], ("dp", "fsdp"), axis=0, tiled=True),
            lax.all_gather(shards[5], ("dp", "fsdp"), axis=0, tiled=True),
            lax.all_gather(shards[6], ("dp", "fsdp"), axis=0, tiled=True),
            lax.all_gather(shards[7], ("dp", "fsdp"), axis=0, tiled=True),
            lax.all_gather(shards[8], ("dp", "fsdp"), axis=0, tiled=True),
            lax.all_gather(shards[9], ("dp", "fsdp"), axis=0, tiled=True),
            lax.all_gather(shards[10], ("dp", "fsdp"), axis=0, tiled=True),
            lax.all_gather(shards[11], ("dp", "fsdp"), axis=0, tiled=True),
        )
        (
            qkv_mat,
            qkv_bias,
            out_mat,
            out_bias,
            gain_one,
            bias_one,
            up_mat,
            up_bias,
            down_mat,
            down_bias,
            gain_two,
            bias_two,
        ) = unpack(fetched)
        seq_len = lax.dynamic_slice_in_dim(lengths[micro_idx], dp_place * seq_dp, seq_dp)
        visible = key_places[None, :] < seq_len[:, None]
        block_in = work_in[micro_idx].reshape(row_total, D)
        projected = jnp.dot(block_in, qkv_mat, preferred_element_type=jnp.float32) + qkv_bias
        queries = rotate(
            projected[:, :D].reshape(seq_dp, local_rows, D), query_places, False
        ).astype(jnp.bfloat16)
        keys_local = rotate(
            projected[:, D : 2 * D].reshape(seq_dp, local_rows, D), query_places, False
        ).astype(jnp.bfloat16)
        values_local = projected[:, 2 * D :].reshape(seq_dp, local_rows, D).astype(jnp.bfloat16)
        keys_all, values_all = (
            lax.all_gather(keys_local, "fsdp", axis=1, tiled=True),
            lax.all_gather(values_local, "fsdp", axis=1, tiled=True),
        )
        query_heads = queries.reshape(seq_dp, local_rows, HEADS, HD)
        key_heads = keys_all.reshape(seq_dp, full_len, HEADS, HD)
        value_heads = values_all.reshape(seq_dp, full_len, HEADS, HD)
        scores = (
            jnp.einsum(
                "sqhd,skhd->shqk", query_heads, key_heads, preferred_element_type=jnp.float32
            )
            * scale
        )
        scores = jnp.where(visible[:, None, None, :], scores, -1000000000.0)
        peak = jnp.max(scores, axis=-1, keepdims=True)
        expanded = jnp.exp(scores - peak)
        row_total_exp = jnp.sum(expanded, axis=-1, keepdims=True)
        probabilities = expanded / row_total_exp
        log_total = peak + jnp.log(row_total_exp)
        attended = jnp.einsum(
            "shqk,skhd->sqhd",
            probabilities.astype(jnp.bfloat16),
            value_heads,
            preferred_element_type=jnp.float32,
        )
        merged = attended.reshape(row_total, D).astype(jnp.bfloat16)
        branch = jnp.dot(merged, out_mat, preferred_element_type=jnp.float32) + out_bias
        normed, standard_one, inverse_one = normalize(
            block_in.astype(jnp.float32) + branch, gain_one, bias_one
        )
        normed_low = normed.astype(jnp.bfloat16)
        hidden = jnp.dot(normed_low, up_mat, preferred_element_type=jnp.float32) + up_bias
        active_low = jax.nn.gelu(hidden, approximate=False).astype(jnp.bfloat16)
        down_out = jnp.dot(active_low, down_mat, preferred_element_type=jnp.float32) + down_bias
        result, standard_two, inverse_two = normalize(normed + down_out, gain_two, bias_two)
        outputs_list.append(result.astype(jnp.bfloat16).reshape(seq_dp, local_rows, D))
        fetched = (
            lax.all_gather(shards[0], ("dp", "fsdp"), axis=0, tiled=True),
            lax.all_gather(shards[1], ("dp", "fsdp"), axis=0, tiled=True),
            lax.all_gather(shards[2], ("dp", "fsdp"), axis=0, tiled=True),
            lax.all_gather(shards[3], ("dp", "fsdp"), axis=0, tiled=True),
            lax.all_gather(shards[4], ("dp", "fsdp"), axis=0, tiled=True),
            lax.all_gather(shards[5], ("dp", "fsdp"), axis=0, tiled=True),
            lax.all_gather(shards[6], ("dp", "fsdp"), axis=0, tiled=True),
            lax.all_gather(shards[7], ("dp", "fsdp"), axis=0, tiled=True),
            lax.all_gather(shards[8], ("dp", "fsdp"), axis=0, tiled=True),
            lax.all_gather(shards[9], ("dp", "fsdp"), axis=0, tiled=True),
            lax.all_gather(shards[10], ("dp", "fsdp"), axis=0, tiled=True),
            lax.all_gather(shards[11], ("dp", "fsdp"), axis=0, tiled=True),
        )
        (
            qkv_mat,
            qkv_bias,
            out_mat,
            out_bias,
            gain_one,
            bias_one,
            up_mat,
            up_bias,
            down_mat,
            down_bias,
            gain_two,
            bias_two,
        ) = unpack(fetched)
        grad_top = work_grad[micro_idx].reshape(row_total, D).astype(jnp.float32)
        grad_two, gain_two_grad, bias_two_grad = normalize_back(
            grad_top, standard_two, inverse_two, gain_two
        )
        down_grad = grad_two.astype(jnp.bfloat16)
        down_bias_grad = jnp.sum(down_grad.astype(jnp.float32), axis=0)
        down_mat_grad = contract_rows(active_low, down_grad)
        hidden_grad = (times_transposed(down_grad, down_mat) * gelu_slope(hidden)).astype(
            jnp.bfloat16
        )
        up_bias_grad = jnp.sum(hidden_grad.astype(jnp.float32), axis=0)
        up_mat_grad = contract_rows(normed_low, hidden_grad)
        normed_grad = grad_two + times_transposed(hidden_grad, up_mat)
        grad_one, gain_one_grad, bias_one_grad = normalize_back(
            normed_grad, standard_one, inverse_one, gain_one
        )
        branch_grad = grad_one.astype(jnp.bfloat16)
        out_bias_grad = jnp.sum(branch_grad.astype(jnp.float32), axis=0)
        out_mat_grad = contract_rows(merged, branch_grad)
        merged_grad = (
            times_transposed(branch_grad, out_mat)
            .astype(jnp.bfloat16)
            .reshape(seq_dp, local_rows, HEADS, HD)
        )
        scores = (
            jnp.einsum(
                "sqhd,skhd->shqk", query_heads, key_heads, preferred_element_type=jnp.float32
            )
            * scale
        )
        scores = jnp.where(visible[:, None, None, :], scores, -1000000000.0)
        probabilities = jnp.exp(scores - log_total)
        prob_grad = jnp.einsum(
            "sqhd,skhd->shqk", merged_grad, value_heads, preferred_element_type=jnp.float32
        )
        row_dot = jnp.sum(prob_grad * probabilities, axis=-1, keepdims=True)
        score_grad = (probabilities * (prob_grad - row_dot)).astype(jnp.bfloat16)
        query_grad = (
            jnp.einsum("shqk,skhd->sqhd", score_grad, key_heads, preferred_element_type=jnp.float32)
            * scale
        )
        values_grad = jnp.einsum(
            "shqk,sqhd->skhd",
            probabilities.astype(jnp.bfloat16),
            merged_grad,
            preferred_element_type=jnp.float32,
        )
        keys_grad = (
            jnp.einsum(
                "shqk,sqhd->skhd", score_grad, query_heads, preferred_element_type=jnp.float32
            )
            * scale
        )
        key_part, value_part = (
            lax.psum_scatter(
                keys_grad.reshape(seq_dp, full_len, D).astype(jnp.bfloat16),
                "fsdp",
                scatter_dimension=1,
                tiled=True,
            ).astype(jnp.float32),
            lax.psum_scatter(
                values_grad.reshape(seq_dp, full_len, D).astype(jnp.bfloat16),
                "fsdp",
                scatter_dimension=1,
                tiled=True,
            ).astype(jnp.float32),
        )
        qkv_grad = jnp.concatenate(
            [
                rotate(query_grad.reshape(seq_dp, local_rows, D), query_places, True),
                rotate(key_part, query_places, True),
                value_part,
            ],
            axis=-1,
        )
        qkv_grad = qkv_grad.reshape(row_total, 3 * D).astype(jnp.bfloat16)
        qkv_bias_grad = jnp.sum(qkv_grad.astype(jnp.float32), axis=0)
        qkv_mat_grad = contract_rows(block_in, qkv_grad)
        input_grad = times_transposed(qkv_grad, qkv_mat) + grad_one
        grads_list.append(input_grad.astype(jnp.bfloat16).reshape(seq_dp, local_rows, D))
        flat_grads = tuple(
            (
                piece.reshape(-1)
                for piece in (
                    qkv_mat_grad,
                    qkv_bias_grad,
                    out_mat_grad,
                    out_bias_grad,
                    gain_one_grad,
                    bias_one_grad,
                    up_mat_grad,
                    up_bias_grad,
                    down_mat_grad,
                    down_bias_grad,
                    gain_two_grad,
                    bias_two_grad,
                )
            )
        )
        if micro_idx == 0:
            accumulated = flat_grads
        else:
            accumulated = tuple(
                (old_part + new_part for old_part, new_part in zip(accumulated, flat_grads))
            )
    owned = lax.psum_scatter(accumulated, ("dp", "fsdp"), scatter_dimension=0, tiled=True)
    results = jnp.stack(outputs_list)
    input_grads = jnp.stack(grads_list)
    back_out, back_grad = (
        lax.all_to_all(results, "dp", split_axis=2, concat_axis=1, tiled=True),
        lax.all_to_all(input_grads, "dp", split_axis=2, concat_axis=1, tiled=True),
    )
    inverses = [jnp.argsort(deal[micro_idx]) for micro_idx in range(batches)]
    home_out = jnp.stack([back_out[micro_idx][inverses[micro_idx]] for micro_idx in range(batches)])
    home_grad = jnp.stack(
        [back_grad[micro_idx][inverses[micro_idx]] for micro_idx in range(batches)]
    )
    return (
        home_out,
        home_grad,
        owned[0],
        owned[1],
        owned[2],
        owned[3],
        owned[4],
        owned[5],
        owned[6],
        owned[7],
        owned[8],
        owned[9],
        owned[10],
        owned[11],
    )


def solution(mesh):
    in_specs = (
        P(None, None, ("dp", "fsdp"), None),
        P(),
        P(),
        P(("dp", "fsdp")),
        P(("dp", "fsdp")),
        P(("dp", "fsdp")),
        P(("dp", "fsdp")),
        P(("dp", "fsdp")),
        P(("dp", "fsdp")),
        P(("dp", "fsdp")),
        P(("dp", "fsdp")),
        P(("dp", "fsdp")),
        P(("dp", "fsdp")),
        P(("dp", "fsdp")),
        P(("dp", "fsdp")),
        P(None, None, ("dp", "fsdp"), None),
    )
    out_specs = (
        P(None, None, ("dp", "fsdp"), None),
        P(None, None, ("dp", "fsdp"), None),
        P(("dp", "fsdp")),
        P(("dp", "fsdp")),
        P(("dp", "fsdp")),
        P(("dp", "fsdp")),
        P(("dp", "fsdp")),
        P(("dp", "fsdp")),
        P(("dp", "fsdp")),
        P(("dp", "fsdp")),
        P(("dp", "fsdp")),
        P(("dp", "fsdp")),
        P(("dp", "fsdp")),
        P(("dp", "fsdp")),
    )
    return jax.shard_map(body, mesh=mesh, in_specs=in_specs, out_specs=out_specs, check_vma=False)
```

profile of v0, /device:TPU:0, one launch (start us, length us, event | category | flops | bytes accessed | tf_op | source)
XLA Modules:
  0.0 1192.9 jit_solution(1376294809754350054)
XLA Ops:
  14.2 7.3 all-to-all-start
  23.4 42.8 %all-reduce.22 = (bf16[3072]{0:T(1024)(128)(2,1)}, bf16[2304]{0:T(1024)(128)(2,1)S(1)}, bf16[768]{0:T(1024)(128)(2,1)}, bf16[768]{0:T(1024)(128)(2,1)S(1)}, bf16...) all-reduce(bf16[3072]{0:T(1024)(128)(2,1)S(1)} %dynamic-update-slic, ...), channel_id=1, replica_groups=mesh['dp'=8,'fsdp'=4] {'dp','fsdp'}, use_global_device_ids=true, to_apply=%add.4 | all-reduce | flops 9984 | bytes 39936
  67.2 10.8 all-gather.11.cloned.1.call-done
  78.0 7.6 reshape.941
  132.9 13.1 %all-to-all-done.2 = bf16[2,8,32,768]{3,2,0,1:T(8,128)(2,1)S(1)} async-done(((bf16[2,8,32,768]{3,2,0,1:T(8,128)(2,1)}), bf16[2,8,32,768]{3,2,0,1:T(8,128)(2,1)S(1)}, u32[]{:S(2)}, u32[]{:S(2)}) %all-to-all-start.2) | async-done | bytes 786464 | tf_op jit(solution)/shard_map/all_to_all | solution.py:144
  158.3 46.5 %all-gather.17.cloned.1.call-done = bf16[2359296]{0:T(1024)(128)(2,1)} async-done(((bf16[73728]{0:T(1024)(128)(2,1)}), bf16[2359296]{0:T(1024)(128)(2,1)}) %all-gather.17.cloned.1.call-update) | async-done | bytes 4718608 | tf_op jit(solution)/shard_map/all_gather | solution.py:168
  204.8 8.2 reshape.945
  213.0 57.0 %all-gather.19.cloned.1.call-done = bf16[2359296]{0:T(1024)(128)(2,1)} async-done(((bf16[73728]{0:T(1024)(128)(2,1)}), bf16[2359296]{0:T(1024)(128)(2,1)}) %all-gather.19.cloned.1.call-update) | async-done | bytes 4718608 | tf_op jit(solution)/shard_map/all_gather | solution.py:170
  270.0 9.3 reshape.946
  279.2 10.8 all-gather.13.cloned.1.call-done
  301.0 10.8 all-gather.23.cloned.1.call-done
  314.3 6.8 fusion.59
  322.1 11.8 fusion.18
  345.1 9.3 all-gather.25.cloned.1.call-done
  357.0 6.9 fusion.58
  364.9 10.0 fusion.21
  396.8 11.3 multiply_reduce_fusion
  409.6 7.1 multiply_convert_fusion
  425.5 12.3 %multiply_reduce_fusion.1 = (f32[12,256]{1,0:T(8,128)S(1)}, f32[12,256,1024]{2,1,0:T(8,128)}) fusion(f32[12,256]{1,0:T(8,128)S(1)} %log_add_fusion.1, f32[12,256,1024]{2,1,0:T(8,128)} %copy-done.1, pred[1024]{0:T(1024)(128)(4,1)S(1)} %copy-done.78, bf16[256,12,64]{0,2,1:T(8,128)(2,1)S(1)} %bitcast.312, bf16[1024,12,64]{0,2,1:T(8,128)(2,1)S(1)} %bitcast.273), kind=kOutput, calls=%fused_computation.14 | convolution fusion | flops 418378752 | bytes 27157504 | tf_op jit(solution)/shard_map/sqhd,skhd->shqk/dot_general | solution.py:296
  439.0 6.7 multiply_convert_fusion.1
  471.5 9.7 copy.142
  487.9 11.0 add.511
  510.1 7.6 fusion.47
  517.8 32.5 %reshape_bitcast_fusion = bf16[1,256,768]{0,2,1:T(8,128)(2,1)} fusion(bf16[256,768]{1,0:T(8,128)(2,1)} %reduce-scatter.15.cloned.1.call-done), kind=kLoop, calls=%fused_computation.8 | loop fusion | bytes 786432
  550.4 45.6 %copy.129 = bf16[1,256,768]{1,0,2:T(2,128)(2,1)} copy(bf16[1,256,768]{0,2,1:T(8,128)(2,1)} %reshape_bitcast_fusion) | data formatting | bytes 786432
  597.9 32.3 %reshape_bitcast_fusion.1 = bf16[1,256,768]{0,2,1:T(8,128)(2,1)} fusion(bf16[256,768]{1,0:T(8,128)(2,1)} %reduce-scatter.13.cloned.1.call-done), kind=kLoop, calls=%fused_computation.9 | loop fusion | bytes 786432
  630.2 45.6 %copy.127 = bf16[1,256,768]{1,0,2:T(2,128)(2,1)} copy(bf16[1,256,768]{0,2,1:T(8,128)(2,1)} %reshape_bitcast_fusion.1) | data formatting | bytes 786432
  697.5 7.4 convolution_add_fusion
  704.8 8.2 add.500
  728.5 22.2 %all-to-all-done.1 = bf16[2,1,256,768]{3,0,1,2:T(2,128)(2,1)S(1)} async-done(((bf16[2,1,256,768]{3,0,1,2:T(2,128)(2,1)}), bf16[2,1,256,768]{3,0,1,2:T(2,128)(2,1)S(1)}, u32[]{:S(2)}, u32[]{:S(2)}) %all-to-all-start.1) | async-done | bytes 786464 | tf_op jit(solution)/shard_map/all_to_all | solution.py:373
  775.4 42.1 %all-reduce.20 = (f32[2304]{0:T(1024)S(1)}, f32[768]{0:T(1024)S(1)}, f32[768]{0:T(1024)S(1)}, f32[768]{0:T(1024)S(1)}, f32[3072]{0:T(1024)S(1)}, /*index=5*/f32[...) all-reduce(f32[2304]{0:T(1024)S(1)} %add.501, ...), channel_id=9, replica_groups=mesh['dp'=8,'fsdp'=4] {'dp','fsdp'}, use_global_device_ids=true, to_apply=%region_31.32.clone | all-reduce | flops 9984 | bytes 79872
  825.8 353.7 %all-reduce.25.cloned.1.call-done = (f32[1769472]{0:T(1024)}, f32[589824]{0:T(1024)}, f32[2359296]{0:T(1024)}, f32[2359296]{0:T(1024)}) async-done(((f32[1769472]{0:T(1024)}, f32[589824]{0:T(1024)}, f32[2359296]{0:T(1024)}, f32[2359296]{0:T(1024)}), (f32[1769472]{0:T(1024)}, f32[589824]{0:T(1024)}, f32[2359296]{0:T(1024)}, f32[2359296]{0:T(1024)})) %all-reduce.25.cloned.1.call-update) | async-done | bytes 28311568
  (463 shorter events, 252.6 us)
Async XLA Ops:
  7.2 70.8 %all-gather.11.cloned.1.call-start = ((), (), s32[]{:S(2)}) async-start(), calls=%async_computation.8 | async-start | bytes 3649536 | tf_op jit(solution)/shard_map/all_gather | solution.py:162
  7.9 140.2 %all-gather.15.cloned.1.call-start = ((), (), s32[]{:S(2)}) async-start(), calls=%async_computation.10 | async-start | bytes 1216512 | tf_op jit(solution)/shard_map/all_gather | solution.py:164
  8.7 196.1 %all-gather.17.cloned.1.call-start = ((), (), s32[]{:S(2)}) async-start(), calls=%async_computation.11 | async-start | bytes 4866048 | tf_op jit(solution)/shard_map/all_gather | solution.py:168
  9.4 260.6 %all-gather.19.cloned.1.call-start = ((), (), s32[]{:S(2)}) async-start(), calls=%async_computation.12 | async-start | bytes 4866048 | tf_op jit(solution)/shard_map/all_gather | solution.py:170
  14.2 53.0 %all-to-all-start = ((bf16[2,8,32,768]{3,2,0,1:T(8,128)(2,1)}), bf16[2,8,32,768]{3,2,0,1:T(8,128)(2,1)S(1)}, u32[]{:S(2)}, u32[]{:S(2)}) async-start(bf16[2,8,32,768]{3,2,0,1:T(8,128)(2,1)} %pad_maximum_fusion.2), calls=%async_computation | async-start | bytes 1572864 | tf_op jit(solution)/shard_map/all_to_all | solution.py:143
  21.4 268.6 %all-gather.13.cloned.1.call-start = ((), (), s32[]{:S(2)}) async-start(), calls=%async_computation.9 | async-start | bytes 1966080 | tf_op jit(solution)/shard_map/all_gather | solution.py:201
  67.2 18.4 %copy-start.16 = (bf16[1,8,32,768]{3,2,0,1:T(8,128)(2,1)}, bf16[1,8,32,768]{3,2,0,1:T(8,128)(2,1)S(1)}, u32[]{:S(2)}) copy-start(bf16[1,8,32,768]{3,2,0,1:T(8,128)(2,1)S(1)} %get-tuple-element.98) | copy-start | bytes 1179652
  67.2 254.0 %copy-start.21 = (bf16[1,8,32,768]{3,2,0,1:T(8,128)(2,1)}, bf16[1,8,32,768]{3,2,0,1:T(8,128)(2,1)S(1)}, u32[]{:S(2)}) copy-start(bf16[1,8,32,768]{3,2,0,1:T(8,128)(2,1)S(1)} %get-tuple-element.97) | copy-start | bytes 1179652
  114.1 197.6 %all-gather.23.cloned.1.call-start = ((), (), s32[]{:S(2)}) async-start(), calls=%async_computation.16 | async-start | bytes 1966080 | tf_op jit(solution)/shard_map/all_gather | solution.py:202
  116.1 220.3 %all-gather.21.cloned.1.call-start = ((), (), s32[]{:S(2)}) async-start(), calls=%async_computation.13 | async-start | bytes 1966080 | tf_op jit(solution)/shard_map/all_gather | solution.py:201
  120.2 32.5 %copy-start.45 = (bf16[1,256,12,32,1]{1,4,3,2,0:T(2,128)(2,1)S(1)}, bf16[1,256,12,32,1]{1,4,3,2,0:T(2,128)(2,1)}, u32[]{:S(2)}) copy-start(bf16[1,256,12,32,1]{1,4,3,2,0:T(2,128)(2,1)} %get-tuple-element.107) | copy-start | bytes 589828
  120.2 25.8 %all-to-all-start.2 = ((bf16[2,8,32,768]{3,2,0,1:T(8,128)(2,1)}), bf16[2,8,32,768]{3,2,0,1:T(8,128)(2,1)S(1)}, u32[]{:S(2)}, u32[]{:S(2)}) async-start(bf16[2,8,32,768]{3,2,0,1:T(8,128)(2,1)} %pad_maximum_fusion.5), calls=%async_computation.2 | async-start | bytes 1572864 | tf_op jit(solution)/shard_map/all_to_all | solution.py:144
  124.1 33.1 %copy-start.44 = (bf16[1,256,12,32,1]{1,4,3,2,0:T(2,128)(2,1)S(1)}, bf16[1,256,12,32,1]{1,4,3,2,0:T(2,128)(2,1)}, u32[]{:S(2)}) copy-start(bf16[1,256,12,32,1]{1,4,3,2,0:T(2,128)(2,1)} %get-tuple-element.112) | copy-start | bytes 589828
  124.1 230.3 %all-gather.25.cloned.1.call-start = ((), (), s32[]{:S(2)}) async-start(), calls=%async_computation.17 | async-start | bytes 1966080 | tf_op jit(solution)/shard_map/all_gather | solution.py:202
  158.2 131.8 %copy-start.13 = (bf16[256,12,64]{0,2,1:T(8,128)(2,1)}, bf16[256,12,64]{0,2,1:T(8,128)(2,1)S(1)}, u32[]{:S(2)}) copy-start(bf16[256,12,64]{0,2,1:T(8,128)(2,1)S(1)} %convert_element_type.361) | copy-start | bytes 1179652
  158.3 359.6 %reduce-scatter.15.cloned.1.call-start = ((), (), s32[]{:S(2)}) async-start(), calls=%async_computation.19 | async-start | bytes 1966080
  213.0 77.1 %copy-start.77 = (pred[1024]{0:T(1024)(128)(4,1)S(1)}, pred[1024]{0:T(1024)(128)(4,1)}, u32[]{:S(2)}) copy-start(pred[1024]{0:T(1024)(128)(4,1)} %broadcast_compare_fusion.1) | copy-start | bytes 3076
  293.4 20.9 %copy-start.59 = (f32[12,256]{1,0:T(8,128)}, f32[12,256]{1,0:T(8,128)S(1)}, u32[]{:S(2)}) copy-start(f32[12,256]{1,0:T(8,128)S(1)} %get-tuple-element.126) | copy-start | bytes 36868
  300.9 20.2 %copy-start.62 = (f32[12,256]{1,0:T(8,128)}, f32[12,256]{1,0:T(8,128)S(1)}, u32[]{:S(2)}) copy-start(f32[12,256]{1,0:T(8,128)S(1)} %fusion) | copy-start | bytes 36868
  357.0 17.8 %slice-start.13 = ((s8[4718592]{0:T(1024)(128)(4,1)}), s8[4194304]{0:T(1024)(128)(4,1)S(1)}, s32[]{:S(2)}) async-start(s8[4718592]{0:T(1024)(128)(4,1)} %bitcast.283), calls=%async_computation.34 | async-start | bytes 8388608
  364.8 27.0 %copy-start.63 = (f32[256]{0:T(256)}, f32[256]{0:T(256)S(1)}, u32[]{:S(2)}) copy-start(f32[256]{0:T(256)S(1)} %add_rsqrt_fusion.1) | copy-start | bytes 3076
  420.9 177.0 %reduce-scatter.13.cloned.1.call-start = ((), (), s32[]{:S(2)}) async-start(), calls=%async_computation.18 | async-start | bytes 1966080
  425.5 13.4 %slice-start.5 = ((s8[12582912]{0:T(1024)(128)(4,1)}), s8[4194304]{0:T(1024)(128)(4,1)S(1)}, s32[]{:S(2)}) async-start(s8[12582912]{0:T(1024)(128)(4,1)} %bitcast.261), calls=%async_computation.26 | async-start | bytes 8388608
  449.9 242.5 %reduce-scatter.9.cloned.1.call-start = ((), (), s32[]{:S(2)}) async-start(), calls=%async_computation.14 | async-start | bytes 1966080 | tf_op jit(solution)/shard_map/reduce_scatter | solution.py:324
  466.1 231.4 %reduce-scatter.11.cloned.1.call-start = ((), (), s32[]{:S(2)}) async-start(), calls=%async_computation.15 | async-start | bytes 1966080 | tf_op jit(solution)/shard_map/reduce_scatter | solution.py:324
  517.8 661.7 %all-reduce.25.cloned.1.call-start = ((), (), s32[]{:S(2)}) async-start(), calls=%async_computation.20 | async-start | bytes 56623104
  716.0 34.7 %all-to-all-start.1 = ((bf16[2,1,256,768]{3,0,1,2:T(2,128)(2,1)}), bf16[2,1,256,768]{3,0,1,2:T(2,128)(2,1)S(1)}, u32[]{:S(2)}, u32[]{:S(2)}) async-start(bf16[2,1,256,768]{3,0,1,2:T(2,128)(2,1)} %copy.112), calls=%async_computation.1 | async-start | bytes 1572864 | tf_op jit(solution)/shard_map/all_to_all | solution.py:373
  726.7 32.1 %copy-start.67 = (f32[768]{0:T(1024)S(1)}, f32[768]{0:T(1024)}, u32[]{:S(2)}) copy-start(f32[768]{0:T(1024)} %get-tuple-element.32) | copy-start | bytes 9220
  726.7 32.1 %copy-start.68 = (f32[768]{0:T(1024)S(1)}, f32[768]{0:T(1024)}, u32[]{:S(2)}) copy-start(f32[768]{0:T(1024)} %get-tuple-element.33) | copy-start | bytes 9220
  726.7 32.7 %copy-start.69 = (f32[768]{0:T(1024)S(1)}, f32[768]{0:T(1024)}, u32[]{:S(2)}) copy-start(f32[768]{0:T(1024)} %get-tuple-element.20) | copy-start | bytes 9220
  726.7 32.7 %copy-start.70 = (f32[768]{0:T(1024)S(1)}, f32[768]{0:T(1024)}, u32[]{:S(2)}) copy-start(f32[768]{0:T(1024)} %get-tuple-element.29) | copy-start | bytes 9220
  750.7 71.5 %all-to-all-start.3 = ((bf16[2,1,256,768]{3,0,1,2:T(2,128)(2,1)}), bf16[2,1,256,768]{3,0,1,2:T(2,128)(2,1)S(1)}, u32[]{:S(2)}, u32[]{:S(2)}) async-start(bf16[2,1,256,768]{3,0,1,2:T(2,128)(2,1)} %copy.123), calls=%async_computation.5 | async-start | bytes 1572864 | tf_op jit(solution)/shard_map/all_to_all | solution.py:374
  (99 other events, 626.9 us)
Sparse Core Ops, SparseCore 0:
  10.9 67.0 all-gather.10
  80.9 54.7 all-gather.14
  138.6 66.1 all-gather.16
  207.5 62.3 all-gather.18
  271.4 18.6 all-gather.12
  292.0 19.6 all-gather.22
  313.3 19.8 all-gather.20
  334.7 19.6 all-gather.24
  421.1 28.1 reduce-scatter.14
  451.8 28.1 reduce-scatter.12
  482.6 28.1 reduce-scatter.8
  517.9 28.3 reduce-scatter.10
  713.1 466.2 all-reduce.24
where the time goes:
time: 1200 us; the launch traced here: 1190 us
  waiting for transfers between devices  537 us (45%)
  local copies, waits for them, and re-layouts  298 us (25%)
  matrix products  153 us (13%)
  blocking collectives  85 us (7%)
  other arithmetic  81.3 us (7%)
  starting transfers between devices  22.1 us (2%)
  between operations  16 us (1%)
    unnamed x16, waiting for transfers between devices  356 us
    unnamed x267, local copies, waits for them, and re-layouts  199 us
    unnamed x2, blocking collectives  85 us
    all_gather x1, waiting for transfers between devices, body(): lax.all_gather(shards[8], ('dp', 'fsdp'), axis=0, tiled=True)  57 us
    all_gather x1, waiting for transfers between devices, body(): lax.all_gather(shards[6], ('dp', 'fsdp'), axis=0, tiled=True)  46.5 us
    dot_general x8, matrix products, contract_rows(): lax.dot_general(left, right, (((0,), (0,)), ((), ())), preferred_element_...  32.6 us
  transfers between devices with their start and end apart: 17, of which 9 were waited for; matrix products, arithmetic and copies ran while one was open for 36% of the time, Pallas kernels for 0%

commit v1 on v0

v1 whole, which is shorter than its diff:
```python
import math

import jax
import jax.numpy as jnp
from jax import lax
from jax.sharding import PartitionSpec as P

D = 768
HEADS = 12
HD = 64
FF = 3072
AXES = ("dp", "fsdp")
F32 = jnp.float32
BF16 = jnp.bfloat16


class Plan:
    def __init__(self, n_dp, n_fsdp):
        self.n = n_dp * n_fsdp
        self.chips = self.n // 2
        bits = [1 << k for k in range(1, self.n.bit_length() - 1)]
        near, far = bits[:2], bits[2:]
        first = [b | (b >> 1) if b >> 1 in far else b for b in reversed(far)]
        self.masks = [first + near[::-1], first + near]
        self.levels = len(bits)
        self.combos = []
        for masks in self.masks:
            row = []
            for rel in range(self.chips):
                total = 0
                for k in range(self.levels):
                    if rel >> k & 1:
                        total ^= masks[k]
                row.append(total)
            self.combos.append(row)

    def pairs(self, level):
        return [(i, i ^ self.masks[i & 1][level]) for i in range(self.n)]

    def core_pairs(self):
        return [(i, i ^ 1) for i in range(self.n)]

    def order(self, me, core):
        table = jnp.asarray(self.combos, jnp.int32)
        return (me ^ jnp.where(core == 0, table[0], table[1])) // 2


def swap(value, pairs):
    return lax.ppermute(value, AXES, pairs)


def gather_chips(plan, piece):
    held = piece[None]
    for level in range(plan.levels):
        held = jnp.concatenate([held, swap(held, plan.pairs(level))], axis=0)
    return held


def reduce_chips(plan, pieces):
    held = pieces
    for level in reversed(range(plan.levels)):
        half = held.shape[0] // 2
        got = swap(held[half:].astype(BF16), plan.pairs(level))
        held = held[:half].astype(F32) + got.astype(F32)
        if level > 0:
            held = held.astype(BF16)
    return held[0]


def split_columns(plan, core, shard):
    half = shard.shape[1] // 2
    left, right = shard[:, :half], shard[:, half:]
    keep = jnp.where(core == 0, left, right)
    got = swap(jnp.where(core == 0, right, left), plan.core_pairs())
    return jnp.where(core == 0, jnp.concatenate([keep, got], 0), jnp.concatenate([got, keep], 0))


def unsplit_columns(plan, core, block):
    rows = block.shape[0] // 2
    upper, lower = block[:rows], block[rows:]
    keep = jnp.where(core == 0, upper, lower)
    got = swap(jnp.where(core == 0, lower, upper), plan.core_pairs())
    return jnp.where(core == 0, jnp.concatenate([keep, got], 1), jnp.concatenate([got, keep], 1))


def rotate(values_in, places, backward):
    half_dim = HD // 2
    frequency = 10000.0 ** (-(2.0 * jnp.arange(half_dim, dtype=F32)) / HD)
    angles = places.astype(F32)[:, None] * frequency[None, :]
    cosine = jnp.cos(angles)[:, None, :]
    sine_part = jnp.sin(angles)[:, None, :]
    if backward:
        sine_part = -sine_part
    shaped = values_in.reshape(values_in.shape[0], HEADS, half_dim, 2)
    even_part = shaped[..., 0]
    odd_part = shaped[..., 1]
    turned = jnp.stack(
        [even_part * cosine - odd_part * sine_part, even_part * sine_part + odd_part * cosine],
        axis=-1,
    )
    return turned.reshape(values_in.shape)


def normalize(row_data, norm_gain, offset):
    average = jnp.mean(row_data, axis=-1, keepdims=True)
    centered = row_data - average
    variance = jnp.mean(centered * centered, axis=-1, keepdims=True)
    inverse = lax.rsqrt(variance + 1e-05)
    standard = centered * inverse
    return (standard * norm_gain + offset, standard, inverse)


def normalize_back(grad_out, standard, inverse, norm_gain):
    grad_std = grad_out * norm_gain
    mean_grad = jnp.mean(grad_std, axis=-1, keepdims=True)
    mean_proj = jnp.mean(grad_std * standard, axis=-1, keepdims=True)
    grad_in = inverse * (grad_std - mean_grad - standard * mean_proj)
    return (grad_in, jnp.sum(grad_out * standard, axis=0), jnp.sum(grad_out, axis=0))


def gelu_slope(hidden):
    cumulative = 0.5 * (1.0 + lax.erf(hidden * (1.0 / math.sqrt(2.0))))
    return cumulative + hidden * jnp.exp(-0.5 * hidden * hidden) * (1.0 / math.sqrt(2.0 * math.pi))


def contract_rows(left, right):
    return lax.dot_general(left, right, (((0,), (0,)), ((), ())), preferred_element_type=F32)


def times_transposed(left, right):
    return lax.dot_general(left, right, (((1,), (1,)), ((), ())), preferred_element_type=F32)


def body(
    tokens,
    lengths,
    deal,
    w_qkv,
    b_qkv,
    w_out,
    b_out,
    norm1_gain,
    norm1_bias,
    w_up,
    b_up,
    w_down,
    b_down,
    norm2_gain,
    norm2_bias,
    cotangent,
):
    n_dp = lax.axis_size("dp")
    n_fsdp = lax.axis_size("fsdp")
    plan = Plan(n_dp, n_fsdp)
    n = plan.n
    dp_place = lax.axis_index("dp")
    fsdp_place = lax.axis_index("fsdp")
    me = dp_place * n_fsdp + fsdp_place
    core = me % 2
    batches, slot_count, home_rows, width = tokens.shape
    group = n_fsdp // batches
    part_rows = home_rows // group
    rows = n * part_rows
    local = fsdp_place % group
    batch_place = fsdp_place // group
    scale = 1.0 / math.sqrt(HD)
    mine = plan.order(me, core)
    other = plan.order(me, 1 - core)
    group_pairs = [
        [(i, i - i % group + (i + k) % group) for i in range(n)] for k in range(1, group)
    ]

    def spread(array):
        parts = array.reshape(batches, slot_count, group, part_rows, width)
        parts = parts.transpose(1, 0, 2, 3, 4).reshape(n, part_rows, width)
        moved = lax.all_to_all(parts, AXES, split_axis=0, concat_axis=0, tiled=True)
        return moved.reshape(rows, width)

    def collect(array):
        parts = array.reshape(n, part_rows, width)
        moved = lax.all_to_all(parts, AXES, split_axis=0, concat_axis=0, tiled=True)
        moved = moved.reshape(slot_count, batches, group, part_rows, width)
        return moved.transpose(1, 0, 2, 3, 4).reshape(batches, slot_count, home_rows, width)

    def fetch_split(shard, columns):
        piece = split_columns(plan, core, shard.reshape(-1, columns))
        own = gather_chips(plan, piece)
        par = swap(own, plan.core_pairs())
        own = own[mine_back].reshape(-1, columns // 2)
        par = par[other_back].reshape(-1, columns // 2)
        return jnp.where(
            core == 0, jnp.concatenate([own, par], 1), jnp.concatenate([par, own], 1)
        )

    def fetch_rows(shard, columns):
        own = gather_chips(plan, shard.reshape(-1, columns))
        par = swap(own, plan.core_pairs())
        own = own[mine_back]
        par = par[other_back]
        both = jnp.where(core == 0, jnp.stack([own, par], 1), jnp.stack([par, own], 1))
        return both.reshape(-1, columns)

    def return_split(grad):
        columns = grad.shape[1]
        blocks = grad.reshape(plan.chips, -1, columns)
        half = columns // 2
        left, right = blocks[..., :half], blocks[..., half:]
        own = jnp.where(core == 0, left, right)[mine].astype(BF16)
        par = jnp.where(core == 0, right, left)[other].astype(BF16)
        got = swap(par, plan.core_pairs())
        total = (own.astype(F32) + got.astype(F32)).astype(BF16)
        return unsplit_columns(plan, core, reduce_chips(plan, total)).reshape(-1)

    def return_rows(grad):
        columns = grad.shape[1]
        blocks = grad.reshape(plan.chips, 2, -1, columns)
        own = jnp.where(core == 0, blocks[:, 0], blocks[:, 1])[mine].astype(BF16)
        par = jnp.where(core == 0, blocks[:, 1], blocks[:, 0])[other].astype(BF16)
        got = swap(par, plan.core_pairs())
        total = (own.astype(F32) + got.astype(F32)).astype(BF16)
        return reduce_chips(plan, total).reshape(-1)

    chip_ids = jnp.arange(plan.chips, dtype=jnp.int32)
    mine_back = jnp.argmax(mine[None, :] == chip_ids[:, None], axis=1).astype(jnp.int32)
    other_back = jnp.argmax(other[None, :] == chip_ids[:, None], axis=1).astype(jnp.int32)

    small_shards = (
        b_qkv,
        b_out,
        norm1_gain,
        norm1_bias,
        b_up,
        b_down,
        norm2_gain,
        norm2_bias,
    )
    sizes = [piece.shape[0] for piece in small_shards]
    packed = jnp.concatenate(small_shards)
    everyone = lax.all_to_all(
        jnp.broadcast_to(packed[None], (n, packed.shape[0])),
        AXES,
        split_axis=0,
        concat_axis=0,
        tiled=True,
    )
    vectors = []
    start = 0
    for size in sizes:
        vectors.append(everyone[:, start : start + size].reshape(-1).astype(F32))
        start += size
    (qkv_bias, out_bias, gain_one, bias_one, up_bias, down_bias, gain_two, bias_two) = vectors

    block_in = spread(tokens)
    qkv_mat = fetch_split(w_qkv, 3 * D)
    out_mat = fetch_split(w_out, D)
    up_mat = fetch_split(w_up, FF)
    down_mat = fetch_rows(w_down, D)
    grad_top = spread(cotangent).astype(F32)

    home_len = jnp.zeros((batches, slot_count), jnp.int32)
    home_len = home_len.at[jnp.arange(batches, dtype=jnp.int32)[:, None], deal].set(lengths)
    seq_len = home_len[batch_place, dp_place]

    row_ids = jnp.arange(rows, dtype=jnp.int32)
    base_places = row_ids // part_rows * home_rows + row_ids % part_rows
    query_places = base_places + local * part_rows
    key_places = jnp.concatenate(
        [base_places + (local + k) % group * part_rows for k in range(group)]
    )
    visible = key_places < seq_len

    projected = jnp.dot(block_in, qkv_mat, preferred_element_type=F32) + qkv_bias
    queries = rotate(projected[:, :D], query_places, False).astype(BF16)
    keys_local = rotate(projected[:, D : 2 * D], query_places, False).astype(BF16)
    values_local = projected[:, 2 * D :].astype(BF16)
    key_value = jnp.concatenate([keys_local, values_local], axis=1)
    back_pairs = [[(b, a) for a, b in pairs] for pairs in group_pairs]
    all_kv = jnp.concatenate([key_value] + [swap(key_value, pairs) for pairs in back_pairs])
    query_heads = queries.reshape(rows, HEADS, HD)
    key_heads = all_kv[:, :D].reshape(-1, HEADS, HD)
    value_heads = all_kv[:, D:].reshape(-1, HEADS, HD)

    def scores_of():
        scores = (
            jnp.einsum("qhd,khd->hqk", query_heads, key_heads, preferred_element_type=F32) * scale
        )
        return jnp.where(visible[None, None, :], scores, -1000000000.0)

    scores = scores_of()
    peak = jnp.max(scores, axis=-1, keepdims=True)
    expanded = jnp.exp(scores - peak)
    row_total_exp = jnp.sum(expanded, axis=-1, keepdims=True)
    probabilities = expanded / row_total_exp
    log_total = peak + jnp.log(row_total_exp)
    attended = jnp.einsum(
        "hqk,khd->qhd", probabilities.astype(BF16), value_heads, preferred_element_type=F32
    )
    merged = attended.reshape(rows, D).astype(BF16)
    branch = jnp.dot(merged, out_mat, preferred_element_type=F32) + out_bias
    normed, standard_one, inverse_one = normalize(
        block_in.astype(F32) + branch, gain_one, bias_one
    )
    normed_low = normed.astype(BF16)
    hidden = jnp.dot(normed_low, up_mat, preferred_element_type=F32) + up_bias
    active_low = jax.nn.gelu(hidden, approximate=False).astype(BF16)
    down_out = jnp.dot(active_low, down_mat, preferred_element_type=F32) + down_bias
    result, standard_two, inverse_two = normalize(normed + down_out, gain_two, bias_two)
    home_out = collect(result.astype(BF16))

    grad_two, gain_two_grad, bias_two_grad = normalize_back(
        grad_top, standard_two, inverse_two, gain_two
    )
    down_grad = grad_two.astype(BF16)
    down_bias_grad = jnp.sum(down_grad.astype(F32), axis=0)
    down_mat_grad = return_rows(contract_rows(active_low, down_grad))
    hidden_grad = (times_transposed(down_grad, down_mat) * gelu_slope(hidden)).astype(BF16)
    up_bias_grad = jnp.sum(hidden_grad.astype(F32), axis=0)
    up_mat_grad = return_split(contract_rows(normed_low, hidden_grad))
    normed_grad = grad_two + times_transposed(hidden_grad, up_mat)
    grad_one, gain_one_grad, bias_one_grad = normalize_back(
        normed_grad, standard_one, inverse_one, gain_one
    )
    branch_grad = grad_one.astype(BF16)
    out_bias_grad = jnp.sum(branch_grad.astype(F32), axis=0)
    out_mat_grad = return_split(contract_rows(merged, branch_grad))
    merged_grad = times_transposed(branch_grad, out_mat).astype(BF16).reshape(rows, HEADS, HD)
    probabilities = jnp.exp(scores_of() - log_total)
    prob_grad = jnp.einsum("qhd,khd->hqk", merged_grad, value_heads, preferred_element_type=F32)
    row_dot = jnp.sum(prob_grad * probabilities, axis=-1, keepdims=True)
    score_grad = (probabilities * (prob_grad - row_dot)).astype(BF16)
    query_grad = (
        jnp.einsum("hqk,khd->qhd", score_grad, key_heads, preferred_element_type=F32) * scale
    )
    values_grad = jnp.einsum(
        "hqk,qhd->khd", probabilities.astype(BF16), merged_grad, preferred_element_type=F32
    )
    keys_grad = (
        jnp.einsum("hqk,qhd->khd", score_grad, query_heads, preferred_element_type=F32) * scale
    )
    both = jnp.concatenate([keys_grad.reshape(-1, D), values_grad.reshape(-1, D)], axis=1)
    kv_part = both[:rows]
    for k in range(1, group):
        kv_part = kv_part + swap(
            both[k * rows : (k + 1) * rows].astype(BF16), group_pairs[k - 1]
        ).astype(F32)
    qkv_grad = jnp.concatenate(
        [
            rotate(query_grad.reshape(rows, D), query_places, True),
            rotate(kv_part[:, :D], query_places, True),
            kv_part[:, D:],
        ],
        axis=-1,
    ).astype(BF16)
    qkv_bias_grad = jnp.sum(qkv_grad.astype(F32), axis=0)
    qkv_mat_grad = return_split(contract_rows(block_in, qkv_grad))
    input_grad = times_transposed(qkv_grad, qkv_mat) + grad_one
    home_grad = collect(input_grad.astype(BF16))

    small_grads = (
        qkv_bias_grad,
        out_bias_grad,
        gain_one_grad,
        bias_one_grad,
        up_bias_grad,
        down_bias_grad,
        gain_two_grad,
        bias_two_grad,
    )
    packed_grads = jnp.concatenate([piece.reshape(n, -1) for piece in small_grads], axis=1)
    got = lax.all_to_all(packed_grads, AXES, split_axis=0, concat_axis=0, tiled=True)
    summed = jnp.sum(got, axis=0)
    owned = []
    start = 0
    for size in sizes:
        owned.append(summed[start : start + size])
        start += size
    return (
        home_out,
        home_grad,
        qkv_mat_grad,
        owned[0],
        out_mat_grad,
        owned[1],
        owned[2],
        owned[3],
        up_mat_grad,
        owned[4],
        down_mat_grad,
        owned[5],
        owned[6],
        owned[7],
    )


def solution(mesh):
    rows = P(None, None, AXES, None)
    flat = P(AXES)
    in_specs = (rows, P(), P()) + (flat,) * 12 + (rows,)
    out_specs = (rows, rows) + (flat,) * 12
    return jax.shard_map(body, mesh=mesh, in_specs=in_specs, out_specs=out_specs, check_vma=False)
```

time: 1200 us -> 558 us (0.47)
  waiting for transfers between devices: 537 us -> 95 us
  local copies, waits for them, and re-layouts: 298 us -> 122 us
  blocking collectives: 85 us -> 0 us
  starting transfers between devices: 22.1 us -> 102 us
  matrix products: 153 us -> 124 us
  other arithmetic: 81.3 us -> 105 us
  between operations: 16 us -> 2.35 us
    unnamed x16 -> x0, waiting for transfers between devices: 356 us -> none
    unnamed x267 -> x128, local copies, waits for them, and re-layouts: 199 us -> 14.4 us
    all_gather x8 -> x0, waiting for transfers between devices: 145 us -> none  [the longest x1 57 us: body(): lax.all_gather(shards[8], ('dp', 'fsdp'), axis=0, tiled=True)]
    ppermute x0 -> x48, waiting for transfers between devices: none -> 95 us  [swap(): return lax.ppermute(value, AXES, pairs)]
    unnamed x2 -> x0, blocking collectives: 85 us -> none
    ppermute x0 -> x48, starting transfers between devices: none -> 68.4 us  [swap(): return lax.ppermute(value, AXES, pairs)]
    gather x8 -> x16, local copies, waits for them, and re-layouts: 7.11 us -> 47 us  [the longest x3 9.83 us: return_split(): own = jnp.where(core == 0, left, right)[mine].astype(BF16)]
    all_to_all x4 -> x6, waiting for transfers between devices: 35.3 us -> 0.02 us  [the longest x2 0.01 us: spread(): moved = lax.all_to_all(parts, AXES, split_axis=0, concat_axis=0, tiled=True)]
  transfers between devices with their start and end apart: 17 -> 54, of which waited for: 9 -> 16; matrix products, arithmetic and copies ran while one was open for 36% -> 42% of each run, Pallas kernels for 0% -> 0%
where the time goes in v1:
time: 558 us; the launch traced here: 551 us
  matrix products  124 us (22%)
  local copies, waits for them, and re-layouts  122 us (22%)
  other arithmetic  105 us (19%)
  starting transfers between devices  102 us (18%)
  waiting for transfers between devices  95 us (17%)
    ppermute x48, waiting for transfers between devices, swap(): return lax.ppermute(value, AXES, pairs)  95 us
    ppermute x48, starting transfers between devices, swap(): return lax.ppermute(value, AXES, pairs)  68.4 us
    dot_general x1, matrix products, body(): jnp.einsum('qhd,khd->hqk', merged_grad, value_heads, preferred_element_ty...  20.7 us
    convert_element_type x1, other arithmetic, body(): score_grad = (probabilities * (prob_grad - row_dot)).astype(BF16)  17.2 us
    dot_general x1, matrix products, body(): hidden = jnp.dot(normed_low, up_mat, preferred_element_type=F32) + up_bias  16.4 us
    unnamed x128, local copies, waits for them, and re-layouts  14.4 us
    dot_general x4, matrix products, contract_rows(): lax.dot_general(left, right, (((0,), (0,)), ((), ())), preferred_element_...  13.2 us
    dot_general x1, matrix products, body(): jnp.einsum('hqk,qhd->khd', probabilities.astype(BF16), merged_grad, prefe...  12.8 us
  transfers between devices with their start and end apart: 54, of which 16 were waited for; matrix products, arithmetic and copies ran while one was open for 42% of the time, Pallas kernels for 0%

profile of v1, /device:TPU:0, one launch (start us, length us, event | category | flops | bytes accessed | tf_op | source)
XLA Modules:
  0.0 550.5 jit_solution(374581059357317271)
XLA Ops:
  2.4 5.4 concatenate.207
  9.9 7.0 %all-to-all-start.1 = ((bf16[32,2,156]{2,1,0:T(2,128)(2,1)}), bf16[32,2,156]{2,1,0:T(2,128)(2,1)S(1)}, u32[]{:S(2)}, u32[]{:S(2)}) async-start(bf16[32,2,156]{2,1,0:T(2,128)(2,1)} %reshape.973), calls=%async_computation.1 | async-start | bytes 65536 | tf_op jit(solution)/shard_map/all_to_all | solution.py:239
  34.4 5.9 %all-to-all-start = ((bf16[32,16,768]{2,1,0:T(8,128)(2,1)}), bf16[32,16,768]{2,1,0:T(8,128)(2,1)}, u32[]{:S(2)}, u32[]{:S(2)}) async-start(bf16[32,16,768]{2,1,0:T(8,128)(2,1)} %bitcast.2), calls=%async_computation | async-start | bytes 1572864 | tf_op jit(solution)/shard_map/all_to_all | solution.py:176
  46.7 11.2 %collective-permute-done.9 = bf16[2,48,384]{2,1,0:T(8,128)(2,1)S(1)} collective-permute-done((bf16[2,48,384]{2,1,0:T(8,128)(2,1)S(1)}, bf16[2,48,384]{2,1,0:T(8,128)(2,1)S(1)}, u32[]{:S(2)}, u32[]{:S(2)}) %collective-permute-start.9) | collective-permute-done | bytes 73760 | tf_op jit(solution)/shard_map/ppermute | solution.py:49
  60.5 9.4 %collective-permute-start.2 = (bf16[2,48,1152]{2,1,0:T(8,128)(2,1)S(1)}, bf16[2,48,1152]{2,1,0:T(8,128)(2,1)S(1)}, u32[]{:S(2)}, u32[]{:S(2)}) collective-permute-start(bf16[2,48,1152]{2,1,0:T(8,128)(2,1)S(1)} %pad_maximum_fusion.17), channel_id=1, source_target_pairs={{0,8},{1,9},{2,10},{3,11},{4,12},{5,13},{6,14},{7,15},{8,0},{9,1},... | collective-permute-start | bytes 663560 | tf_op jit(solution)/shard_map/ppermute | solution.py:49
  70.7 5.5 %collective-permute-done.2 = bf16[2,48,1152]{2,1,0:T(8,128)(2,1)S(1)} collective-permute-done((bf16[2,48,1152]{2,1,0:T(8,128)(2,1)S(1)}, bf16[2,48,1152]{2,1,0:T(8,128)(2,1)S(1)}, u32[]{:S(2)}, u32[]{:S(2)}) %collective-permute-start.2) | collective-permute-done | bytes 221216 | tf_op jit(solution)/shard_map/ppermute | solution.py:49
  80.0 5.7 %collective-permute-done.3 = bf16[4,48,1152]{2,1,0:T(8,128)(2,1)S(1)} collective-permute-done((bf16[4,48,1152]{2,1,0:T(8,128)(2,1)S(1)}, bf16[4,48,1152]{2,1,0:T(8,128)(2,1)S(1)}, u32[]{:S(2)}, u32[]{:S(2)}) %collective-permute-start.3) | collective-permute-done | bytes 442400 | tf_op jit(solution)/shard_map/ppermute | solution.py:49
  89.8 14.0 %collective-permute-done.21 = bf16[4,96,768]{2,1,0:T(8,128)(2,1)S(1)} collective-permute-done((bf16[4,96,768]{2,1,0:T(8,128)(2,1)S(1)}, bf16[4,96,768]{2,1,0:T(8,128)(2,1)S(1)}, u32[]{:S(2)}, u32[]{:S(2)}) %collective-permute-start.21) | collective-permute-done | bytes 589856 | tf_op jit(solution)/shard_map/ppermute | solution.py:49
  107.2 9.2 %collective-permute-done.16 = bf16[4,48,1536]{2,1,0:T(8,128)(2,1)S(1)} collective-permute-done((bf16[4,48,1536]{2,1,0:T(8,128)(2,1)S(1)}, bf16[4,48,1536]{2,1,0:T(8,128)(2,1)S(1)}, u32[]{:S(2)}, u32[]{:S(2)}) %collective-permute-start.16) | collective-permute-done | bytes 589856 | tf_op jit(solution)/shard_map/ppermute | solution.py:49
  129.3 4.8 collective-permute-done.17
  143.0 6.3 %fusion.23 = f32[512,2304]{0,1:T(8,128)S(1)} fusion(bf16[512,768]{1,0:T(8,128)(2,1)} %bitcast.3, f32[2304]{0:T(1024)S(1)} %reshape.821, bf16[768,1152]{1,0:T(8,128)(2,1)S(1)} %bitcast.200, bf16[768,1152]{1,0:T(8,128)(2,1)} %bitcast.198, pred[]{:T(512)S(6)} %eq.29), kind=kOutput, calls=%fused_computation.59 | convolution fusion | flops 1829044224 | bytes 9053185 | tf_op jit(solution)/shard_map/dot_general | solution.py:272
  157.8 5.6 %subtract_convert_fusion.2 = (bf16[512,12,32,1]{0,3,2,1:T(2,128)(2,1)S(1)}, bf16[512,12,32,1]{0,3,2,1:T(2,128)(2,1)S(1)}, bf16[512,12,32,1]{0,3,2,1:T(2,128)(2,1)S(1)}, bf16[512,12,32,1]{0,3,2,1:T(2,128)(2,1)S(1)}) fusion(f32[512,12,32,2]{0,3,2,1:T(2,128)} %reshape.788, f32[512,32]{0,1:T(8,128)S(1)} %get-tuple-element.80, ...), kind=kLoop, calls=%fused_computation.139 | loop fusion | flops 3145728 | bytes 4849664 | tf_op jit(solution)/shard_map/convert.20
  191.4 5.5 %maximum_select_fusion.1 = bf16[16,2,96,768]{3,2,1,0:T(8,128)(2,1)} fusion(bf16[16,1,96,768]{3,2,1,0:T(8,128)(2,1)} %bitcast.181, bf16[16,1,96,768]{3,2,1,0:T(8,128)(2,1)S(1)} %bitcast.180, pred[]{:T(512)S(6)} %eq.29), kind=kLoop, calls=%fused_computation.61 | loop fusion | flops 7077888 | bytes 9437185 | tf_op jit(solution)/shard_map/jit(_where)/select_n | solution.py:200
  203.8 10.6 %fusion.6 = (f32[12,512]{1,0:T(8,128)S(1)}, f32[12,512,1024]{2,1,0:T(8,128)}) fusion(pred[1024]{0:T(1024)(128)(4,1)S(1)} %add_compare_fusion, bf16[512,12,64]{0,2,1:T(8,128)(2,1)S(1)} %copy-done.10, bf16[1024,12,64]{0,2,1:T(8,128)(2,1)S(1)} %bitcast.176), kind=kOutput, calls=%fused_computation.28 | convolution fusion | flops 824174592 | bytes 27550720 | tf_op jit(solution)/shard_map/qhd,khd->hqk/dot_general | solution.py:285
  214.4 11.2 %fusion = f32[12,512]{1,0:T(8,128)S(1)} fusion(f32[12,512]{1,0:T(8,128)S(1)} %get-tuple-element.92, f32[12,512,1024]{2,1,0:T(8,128)} %get-tuple-element.93, pred[1024]{0:T(1024)(128)(4,1)S(1)} %add_compare_fusion), kind=kLoop, calls=%fused_computation.23 | loop fusion | flops 25159680 | bytes 25216000 | tf_op jit(solution)/shard_map/reduce_sum | solution.py:292
  225.7 11.4 %fusion.34 = bf16[12,64,512]{2,1,0:T(8,128)(2,1)S(1)} fusion(bf16[1024,12,64]{0,2,1:T(8,128)(2,1)S(1)} %bitcast.182, f32[12,512]{1,0:T(8,128)S(1)} %fusion, f32[12,512]{1,0:T(8,128)S(1)} %get-tuple-element.92, f32[12,512,1024]{2,1,0:T(8,128)} %get-tuple-element.93, pred[1024]{0:T(1024)(128)(4,1)S(1)} %add_compare_fusion), kind=kOutput, calls=%fused_computation.114 | convolution fusion | flops 837156864 | bytes 27575296 | tf_op jit(solution)/shard_map/hqk,khd->qhd/dot_general | solution.py:295
  239.7 16.4 %fusion.9 = (bf16[512,3072]{1,0:T(8,128)(2,1)S(1)}, f32[512,3072]{1,0:T(8,128)S(1)}) fusion(f32[3072]{0:T(1024)S(1)} %reshape.825, bf16[768,1536]{1,0:T(8,128)(2,1)S(1)} %bitcast.196, bf16[768,1536]{1,0:T(8,128)(2,1)S(1)} %bitcast.194, pred[]{:T(512)S(6)} %eq.29, f32[512,768]{1,0:T(8,128)S(1)} %get-tuple-element.95, f32[768]{0:T(1024)S(1)} %reshape.824, ...), kind=kOutput, calls=%fused_computation.33 | convolution fusion | flops 2542927872 | bytes 15751169 | tf_op jit(solution)/shard_map/dot_general | solution.py:304
  261.6 5.0 convert_reduce_fusion
  274.5 20.7 %multiply_reduce_fusion = (f32[12,512]{1,0:T(8,128)S(1)}, f32[12,512,1024]{2,1,0:T(8,128)}) fusion(f32[12,512]{1,0:T(8,128)S(1)} %log_add_fusion, f32[12,512,1024]{2,1,0:T(8,128)} %get-tuple-element.93, pred[1024]{0:T(1024)(128)(4,1)S(1)} %add_compare_fusion, bf16[512,12,64]{0,2,1:T(8,128)(2,1)S(1)} %bitcast.192, bf16[1024,12,64]{0,2,1:T(8,128)(2,1)S(1)} %bitcast.183), kind=kOutput, calls=%fused_computation.18 | convolution fusion | flops 836757504 | bytes 52741120 | tf_op jit(solution)/shard_map/qhd,khd->hqk/dot_general | solution.py:328
  295.2 12.8 %fusion.2 = f32[12,64,1024]{2,1,0:T(8,128)} fusion(bf16[512,12,64]{0,2,1:T(8,128)(2,1)S(1)} %bitcast.193, f32[12,512]{1,0:T(8,128)S(1)} %log_add_fusion, f32[12,512,1024]{2,1,0:T(8,128)} %get-tuple-element.93, pred[1024]{0:T(1024)(128)(4,1)S(1)} %add_compare_fusion), kind=kOutput, calls=%fused_computation.25 | convolution fusion | flops 830472192 | bytes 29123584 | tf_op jit(solution)/shard_map/hqk,qhd->khd/dot_general | solution.py:334
  311.4 17.2 %multiply_convert_fusion = bf16[12,512,1024]{2,1,0:T(8,128)(2,1)S(1)} fusion(f32[12,512,1024]{2,1,0:T(8,128)} %get-tuple-element.102, f32[12,512]{1,0:T(8,128)S(1)} %get-tuple-element.101, f32[12,512]{1,0:T(8,128)S(1)} %log_add_fusion, f32[12,512,1024]{2,1,0:T(8,128)} %get-tuple-element.93, pred[1024]{0:T(1024)(128)(4,1)S(1)} %add_compare_fusion), kind=kLoop, calls=%fused_computation.17 | loop fusion | flops 37748736 | bytes 62964736 | tf_op jit(solution)/shard_map/convert_element_type | solution.py:330
  328.6 7.7 %multiply_bitcast_fusion = f32[512,12,64]{0,2,1:T(8,128)} fusion(bf16[1024,12,64]{0,2,1:T(8,128)(2,1)} %bitcast.177, bf16[12,512,1024]{2,1,0:T(8,128)(2,1)S(1)} %multiply_convert_fusion), kind=kOutput, calls=%fused_computation.101 | convolution fusion | flops 805699584 | bytes 15728640 | tf_op jit(solution)/shard_map/hqk,khd->qhd/dot_general | solution.py:332
  338.9 7.3 %convolution_multiply_fusion = f32[12,64,1024]{2,1,0:T(8,128)S(1)} fusion(bf16[512,12,64]{0,2,1:T(8,128)(2,1)} %convert_element_type.369, bf16[12,512,1024]{2,1,0:T(8,128)(2,1)} %copy-done), kind=kOutput, calls=%fused_computation.81 | convolution fusion | flops 806092800 | bytes 16515072 | tf_op jit(solution)/shard_map/hqk,qhd->khd/dot_general | solution.py:338
  349.3 4.8 fusion.75
  371.7 4.9 select_bitcast_fusion.1
  380.3 5.5 %collective-permute-done.35 = bf16[1,48,384]{2,1,0:T(8,128)(2,1)S(1)} collective-permute-done((bf16[1,48,384]{2,1,0:T(8,128)(2,1)S(1)}, bf16[1,48,384]{2,1,0:T(8,128)(2,1)S(1)}, u32[]{:S(2)}, u32[]{:S(2)}) %collective-permute-start.35) | collective-permute-done | bytes 36896 | tf_op jit(solution)/shard_map/ppermute | solution.py:49
  415.1 5.5 subtract_convert_fusion.1
  433.5 6.8 %all-to-all-start.5 = ((f32[32,1,312]{2,1,0:T(1,128)}), f32[32,1,312]{2,1,0:T(1,128)S(1)}, u32[]{:S(2)}, u32[]{:S(2)}) async-start(f32[32,1,312]{2,1,0:T(1,128)} %all_to_all.30), calls=%async_computation.5 | async-start | bytes 98304 | tf_op jit(solution)/shard_map/all_to_all | solution.py:370
  467.4 5.6 %all-to-all-start.4 = ((bf16[32,16,768]{2,1,0:T(8,128)(2,1)}), bf16[32,16,768]{2,1,0:T(8,128)(2,1)}, u32[]{:S(2)}, u32[]{:S(2)}) async-start(bf16[32,16,768]{2,1,0:T(8,128)(2,1)} %bitcast.42), calls=%async_computation.4 | async-start | bytes 1572864 | tf_op jit(solution)/shard_map/all_to_all | solution.py:181
  476.7 17.9 %collective-permute-done.38 = bf16[8,48,1536]{2,1,0:T(8,128)(2,1)} collective-permute-done((bf16[8,48,1536]{2,1,0:T(8,128)(2,1)}, bf16[8,48,1536]{2,1,0:T(8,128)(2,1)}, u32[]{:S(2)}, u32[]{:S(2)}) %collective-permute-start.38) | collective-permute-done | bytes 1179680 | tf_op jit(solution)/shard_map/ppermute | solution.py:49
  530.5 5.7 %collective-permute-start.28 = (bf16[2,48,1152]{2,1,0:T(8,128)(2,1)S(1)}, bf16[2,48,1152]{2,1,0:T(8,128)(2,1)S(1)}, u32[]{:S(2)}, u32[]{:S(2)}) collective-permute-start(bf16[2,48,1152]{2,1,0:T(8,128)(2,1)S(1)} %slice.439), channel_id=1, source_target_pairs={{0,8},{1,9},{2,10},{3,11},{4,12},{5,13},{6,14},{7,15},{8,0},{9,1},... | collective-permute-start | bytes 663560 | tf_op jit(solution)/shard_map/ppermute | solution.py:49
  536.2 5.1 collective-permute-done.28
  (410 shorter events, 270.6 us)
Async XLA Ops:
  1.9 38.7 %collective-permute-start = (bf16[24,1152]{1,0:T(8,128)(2,1)S(1)}, bf16[24,1152]{1,0:T(8,128)(2,1)S(1)}, u32[]{:S(2)}, u32[]{:S(2)}) collective-permute-start(bf16[24,1152]{1,0:T(8,128)(2,1)S(1)} %get-tuple-element.67), channel_id=1, source_target_pairs={{0,1},{1,0},{2,3},{3,2},{4,5},{5,4},{6,7},{7,6},{8,9},{9,8},{10,11... | collective-permute-start | bytes 165896 | tf_op jit(solution)/shard_map/ppermute | solution.py:49
  9.9 24.6 %all-to-all-start.1 = ((bf16[32,2,156]{2,1,0:T(2,128)(2,1)}), bf16[32,2,156]{2,1,0:T(2,128)(2,1)S(1)}, u32[]{:S(2)}, u32[]{:S(2)}) async-start(bf16[32,2,156]{2,1,0:T(2,128)(2,1)} %reshape.973), calls=%async_computation.1 | async-start | bytes 65536 | tf_op jit(solution)/shard_map/all_to_all | solution.py:239
  19.0 26.0 %collective-permute-start.13 = (bf16[24,1536]{1,0:T(8,128)(2,1)S(1)}, bf16[24,1536]{1,0:T(8,128)(2,1)S(1)}, u32[]{:S(2)}, u32[]{:S(2)}) collective-permute-start(bf16[24,1536]{1,0:T(8,128)(2,1)S(1)} %get-tuple-element.61), channel_id=1, source_target_pairs={{0,1},{1,0},{2,3},{3,2},{4,5},{5,4},{6,7},{7,6},{8,9},{9,8},{10,11... | collective-permute-start | bytes 221192 | tf_op jit(solution)/shard_map/ppermute | solution.py:49
  20.4 49.5 %collective-permute-start.19 = (bf16[1,96,768]{2,1,0:T(8,128)(2,1)S(1)}, bf16[1,96,768]{2,1,0:T(8,128)(2,1)S(1)}, u32[]{:S(2)}, u32[]{:S(2)}) collective-permute-start(bf16[1,96,768]{2,1,0:T(8,128)(2,1)S(1)} %broadcast_in_dim_reshape.3), channel_id=1, source_target_pairs={{0,24},{1,25},{2,26},{3,27},{4,28},{5,29},{6,30},{7,31},{8,16},{9,... | collective-permute-start | bytes 442376 | tf_op jit(solution)/shard_map/ppermute | solution.py:49
  34.4 104.4 %all-to-all-start = ((bf16[32,16,768]{2,1,0:T(8,128)(2,1)}), bf16[32,16,768]{2,1,0:T(8,128)(2,1)}, u32[]{:S(2)}, u32[]{:S(2)}) async-start(bf16[32,16,768]{2,1,0:T(8,128)(2,1)} %bitcast.2), calls=%async_computation | async-start | bytes 1572864 | tf_op jit(solution)/shard_map/all_to_all | solution.py:176
  40.6 19.8 %collective-permute-start.1 = (bf16[1,48,1152]{2,1,0:T(8,128)(2,1)S(1)}, bf16[1,48,1152]{2,1,0:T(8,128)(2,1)S(1)}, u32[]{:S(2)}, u32[]{:S(2)}) collective-permute-start(bf16[1,48,1152]{2,1,0:T(8,128)(2,1)S(1)} %get-tuple-element.33), channel_id=1, source_target_pairs={{0,24},{1,25},{2,26},{3,27},{4,28},{5,29},{6,30},{7,31},{8,16},{9,... | collective-permute-start | bytes 331784 | tf_op jit(solution)/shard_map/ppermute | solution.py:49
  45.7 32.2 %collective-permute-start.14 = (bf16[1,48,1536]{2,1,0:T(8,128)(2,1)S(1)}, bf16[1,48,1536]{2,1,0:T(8,128)(2,1)S(1)}, u32[]{:S(2)}, u32[]{:S(2)}) collective-permute-start(bf16[1,48,1536]{2,1,0:T(8,128)(2,1)S(1)} %get-tuple-element.35), channel_id=1, source_target_pairs={{0,24},{1,25},{2,26},{3,27},{4,28},{5,29},{6,30},{7,31},{8,16},{9,... | collective-permute-start | bytes 442376 | tf_op jit(solution)/shard_map/ppermute | solution.py:49
  57.9 60.9 %collective-permute-start.10 = (bf16[4,48,384]{2,1,0:T(8,128)(2,1)S(1)}, bf16[4,48,384]{2,1,0:T(8,128)(2,1)S(1)}, u32[]{:S(2)}, u32[]{:S(2)}) collective-permute-start(bf16[4,48,384]{2,1,0:T(8,128)(2,1)S(1)} %pad_maximum_fusion.18), channel_id=1, source_target_pairs={{0,4},{1,3},{2,6},{3,1},{4,0},{5,7},{6,2},{7,5},{8,12},{9,11},{10,... | collective-permute-start | bytes 442376 | tf_op jit(solution)/shard_map/ppermute | solution.py:49
  69.9 17.5 %collective-permute-start.20 = (bf16[2,96,768]{2,1,0:T(8,128)(2,1)S(1)}, bf16[2,96,768]{2,1,0:T(8,128)(2,1)S(1)}, u32[]{:S(2)}, u32[]{:S(2)}) collective-permute-start(bf16[2,96,768]{2,1,0:T(8,128)(2,1)S(1)} %pad_maximum_fusion.16), channel_id=1, source_target_pairs={{0,8},{1,9},{2,10},{3,11},{4,12},{5,13},{6,14},{7,15},{8,0},{9,1},... | collective-permute-start | bytes 884744 | tf_op jit(solution)/shard_map/ppermute | solution.py:49
  85.9 21.2 %collective-permute-start.4 = (bf16[8,48,1152]{2,1,0:T(8,128)(2,1)S(1)}, bf16[8,48,1152]{2,1,0:T(8,128)(2,1)S(1)}, u32[]{:S(2)}, u32[]{:S(2)}) collective-permute-start(bf16[8,48,1152]{2,1,0:T(8,128)(2,1)S(1)} %pad_maximum_fusion.6), channel_id=1, source_target_pairs={{0,2},{1,5},{2,0},{3,7},{4,6},{5,1},{6,4},{7,3},{8,10},{9,13},{10,... | collective-permute-start | bytes 2654216 | tf_op jit(solution)/shard_map/ppermute | solution.py:49
  89.1 27.3 %collective-permute-start.16 = (bf16[4,48,1536]{2,1,0:T(8,128)(2,1)S(1)}, bf16[4,48,1536]{2,1,0:T(8,128)(2,1)S(1)}, u32[]{:S(2)}, u32[]{:S(2)}) collective-permute-start(bf16[4,48,1536]{2,1,0:T(8,128)(2,1)S(1)} %pad_maximum_fusion.11), channel_id=1, source_target_pairs={{0,4},{1,3},{2,6},{3,1},{4,0},{5,7},{6,2},{7,5},{8,12},{9,11},{10,... | collective-permute-start | bytes 1769480 | tf_op jit(solution)/shard_map/ppermute | solution.py:49
  103.9 23.0 %collective-permute-start.22 = (bf16[8,96,768]{2,1,0:T(8,128)(2,1)S(1)}, bf16[8,96,768]{2,1,0:T(8,128)(2,1)}, u32[]{:S(2)}, u32[]{:S(2)}) collective-permute-start(bf16[8,96,768]{2,1,0:T(8,128)(2,1)S(1)} %pad_maximum_fusion.5), channel_id=1, source_target_pairs={{0,2},{1,5},{2,0},{3,7},{4,6},{5,1},{6,4},{7,3},{8,10},{9,13},{10,... | collective-permute-start | bytes 3538952 | tf_op jit(solution)/shard_map/ppermute | solution.py:49
  107.1 29.4 %collective-permute-start.5 = (bf16[16,48,1152]{2,1,0:T(8,128)(2,1)S(1)}, bf16[16,48,1152]{2,1,0:T(8,128)(2,1)}, u32[]{:S(2)}, u32[]{:S(2)}) collective-permute-start(bf16[16,48,1152]{2,1,0:T(8,128)(2,1)S(1)} %constant_dynamic-update-slice_fusion), channel_id=1, source_target_pairs={{0,1},{1,0},{2,3},{3,2},{4,5},{5,4},{6,7},{7,6},{8,9},{9,8},{10,11... | collective-permute-start | bytes 5308424 | tf_op jit(solution)/shard_map/ppermute | solution.py:49
  119.6 51.6 %collective-permute-start.11 = (bf16[8,48,384]{2,1,0:T(8,128)(2,1)}, bf16[8,48,384]{2,1,0:T(8,128)(2,1)}, u32[]{:S(2)}, u32[]{:S(2)}) collective-permute-start(bf16[8,48,384]{2,1,0:T(8,128)(2,1)} %pad_maximum_fusion.14), channel_id=1, source_target_pairs={{0,2},{1,5},{2,0},{3,7},{4,6},{5,1},{6,4},{7,3},{8,10},{9,13},{10,... | collective-permute-start | bytes 884744 | tf_op jit(solution)/shard_map/ppermute | solution.py:49
  129.3 58.4 %collective-permute-start.23 = (bf16[16,96,768]{2,1,0:T(8,128)(2,1)}, bf16[16,96,768]{2,1,0:T(8,128)(2,1)}, u32[]{:S(2)}, u32[]{:S(2)}) collective-permute-start(bf16[16,96,768]{2,1,0:T(8,128)(2,1)} %constant_dynamic-update-slice_fusion.15), channel_id=1, source_target_pairs={{0,1},{1,0},{2,3},{3,2},{4,5},{5,4},{6,7},{7,6},{8,9},{9,8},{10,11... | collective-permute-start | bytes 7077896 | tf_op jit(solution)/shard_map/ppermute | solution.py:49
  136.5 60.5 %collective-permute-start.18 = (bf16[16,48,1536]{2,1,0:T(8,128)(2,1)}, bf16[16,48,1536]{2,1,0:T(8,128)(2,1)}, u32[]{:S(2)}, u32[]{:S(2)}) collective-permute-start(bf16[16,48,1536]{2,1,0:T(8,128)(2,1)} %constant_dynamic-update-slice_fusion.10), channel_id=1, source_target_pairs={{0,1},{1,0},{2,3},{3,2},{4,5},{5,4},{6,7},{7,6},{8,9},{9,8},{10,11... | collective-permute-start | bytes 7077896 | tf_op jit(solution)/shard_map/ppermute | solution.py:49
  138.8 38.6 %all-to-all-start.3 = ((bf16[32,16,768]{2,1,0:T(8,128)(2,1)}), bf16[32,16,768]{2,1,0:T(8,128)(2,1)S(1)}, u32[]{:S(2)}, u32[]{:S(2)}) async-start(bf16[32,16,768]{2,1,0:T(8,128)(2,1)} %bitcast.34), calls=%async_computation.3 | async-start | bytes 1572864 | tf_op jit(solution)/shard_map/all_to_all | solution.py:176
  170.9 30.0 %collective-permute-start.6 = (bf16[512,1536]{0,1:T(8,128)(2,1)}, bf16[512,1536]{0,1:T(8,128)(2,1)}, u32[]{:S(2)}, u32[]{:S(2)}) collective-permute-start(bf16[512,1536]{0,1:T(8,128)(2,1)} %pad_maximum_fusion.3), channel_id=1, source_target_pairs={{1,0},{0,1},{3,2},{2,3},{5,4},{4,5},{7,6},{6,7},{9,8},{8,9},{11,10... | collective-permute-start | bytes 4718600 | tf_op jit(solution)/shard_map/ppermute | solution.py:49
  311.2 35.0 %collective-permute-start.31 = (bf16[16,48,384]{2,1,0:T(8,128)(2,1)}, bf16[16,48,384]{2,1,0:T(8,128)(2,1)}, u32[]{:S(2)}, u32[]{:S(2)}) collective-permute-start(bf16[16,48,384]{2,1,0:T(8,128)(2,1)} %gather_fusion.11), channel_id=1, source_target_pairs={{0,1},{1,0},{2,3},{3,2},{4,5},{5,4},{6,7},{7,6},{8,9},{9,8},{10,11... | collective-permute-start | bytes 1769480 | tf_op jit(solution)/shard_map/ppermute | solution.py:49
  363.6 45.3 %collective-permute-start.24 = (bf16[512,1536]{0,1:T(8,128)(2,1)}, bf16[512,1536]{0,1:T(8,128)(2,1)}, u32[]{:S(2)}, u32[]{:S(2)}) collective-permute-start(bf16[512,1536]{0,1:T(8,128)(2,1)} %fusion.26), channel_id=1, source_target_pairs={{0,1},{1,0},{2,3},{3,2},{4,5},{5,4},{6,7},{7,6},{8,9},{9,8},{10,11... | collective-permute-start | bytes 4718600 | tf_op jit(solution)/shard_map/ppermute | solution.py:49
  363.6 43.2 %all-to-all-start.2 = ((bf16[32,16,768]{2,1,0:T(8,128)(2,1)}), bf16[32,16,768]{2,1,0:T(8,128)(2,1)}, u32[]{:S(2)}, u32[]{:S(2)}) async-start(bf16[32,16,768]{2,1,0:T(8,128)(2,1)} %bitcast.191), calls=%async_computation.2 | async-start | bytes 1572864 | tf_op jit(solution)/shard_map/all_to_all | solution.py:181
  367.9 18.0 %collective-permute-start.35 = (bf16[1,48,384]{2,1,0:T(8,128)(2,1)S(1)}, bf16[1,48,384]{2,1,0:T(8,128)(2,1)S(1)}, u32[]{:S(2)}, u32[]{:S(2)}) collective-permute-start(bf16[1,48,384]{2,1,0:T(8,128)(2,1)S(1)} %slice.453), channel_id=1, source_target_pairs={{0,24},{1,25},{2,26},{3,27},{4,28},{5,29},{6,30},{7,31},{8,16},{9,... | collective-permute-start | bytes 110600 | tf_op jit(solution)/shard_map/ppermute | solution.py:49
  380.3 69.2 %collective-permute-start.43 = (bf16[16,96,768]{2,1,0:T(8,128)(2,1)}, bf16[16,96,768]{2,1,0:T(8,128)(2,1)}, u32[]{:S(2)}, u32[]{:S(2)}) collective-permute-start(bf16[16,96,768]{2,1,0:T(8,128)(2,1)} %gather_fusion.15), channel_id=1, source_target_pairs={{0,1},{1,0},{2,3},{3,2},{4,5},{5,4},{6,7},{7,6},{8,9},{9,8},{10,11... | collective-permute-start | bytes 7077896 | tf_op jit(solution)/shard_map/ppermute | solution.py:49
  385.9 20.2 %collective-permute-start.36 = (f32[24,384]{1,0:T(8,128)S(1)}, f32[24,384]{1,0:T(8,128)S(1)}, u32[]{:S(2)}, u32[]{:S(2)}) collective-permute-start(f32[24,384]{1,0:T(8,128)S(1)} %get-tuple-element.70), channel_id=1, source_target_pairs={{0,1},{1,0},{2,3},{3,2},{4,5},{5,4},{6,7},{7,6},{8,9},{9,8},{10,11... | collective-permute-start | bytes 110600 | tf_op jit(solution)/shard_map/ppermute | solution.py:49
  398.3 56.3 %collective-permute-start.37 = (bf16[16,48,1536]{2,1,0:T(8,128)(2,1)}, bf16[16,48,1536]{2,1,0:T(8,128)(2,1)}, u32[]{:S(2)}, u32[]{:S(2)}) collective-permute-start(bf16[16,48,1536]{2,1,0:T(8,128)(2,1)} %gather_fusion.13), channel_id=1, source_target_pairs={{0,1},{1,0},{2,3},{3,2},{4,5},{5,4},{6,7},{7,6},{8,9},{9,8},{10,11... | collective-permute-start | bytes 7077896 | tf_op jit(solution)/shard_map/ppermute | solution.py:49
  433.5 33.9 %all-to-all-start.5 = ((f32[32,1,312]{2,1,0:T(1,128)}), f32[32,1,312]{2,1,0:T(1,128)S(1)}, u32[]{:S(2)}, u32[]{:S(2)}) async-start(f32[32,1,312]{2,1,0:T(1,128)} %all_to_all.30), calls=%async_computation.5 | async-start | bytes 98304 | tf_op jit(solution)/shard_map/all_to_all | solution.py:370
  449.2 50.0 %collective-permute-start.25 = (bf16[16,48,1152]{2,1,0:T(8,128)(2,1)}, bf16[16,48,1152]{2,1,0:T(8,128)(2,1)}, u32[]{:S(2)}, u32[]{:S(2)}) collective-permute-start(bf16[16,48,1152]{2,1,0:T(8,128)(2,1)} %gather_fusion.9), channel_id=1, source_target_pairs={{0,1},{1,0},{2,3},{3,2},{4,5},{5,4},{6,7},{7,6},{8,9},{9,8},{10,11... | collective-permute-start | bytes 5308424 | tf_op jit(solution)/shard_map/ppermute | solution.py:49
  453.0 20.1 %collective-permute-start.44 = (bf16[8,96,768]{2,1,0:T(8,128)(2,1)}, bf16[8,96,768]{2,1,0:T(8,128)(2,1)}, u32[]{:S(2)}, u32[]{:S(2)}) collective-permute-start(bf16[8,96,768]{2,1,0:T(8,128)(2,1)} %slice.471), channel_id=1, source_target_pairs={{0,2},{1,5},{2,0},{3,7},{4,6},{5,1},{6,4},{7,3},{8,10},{9,13},{10,... | collective-permute-start | bytes 3538952 | tf_op jit(solution)/shard_map/ppermute | solution.py:49
  459.2 35.4 %collective-permute-start.38 = (bf16[8,48,1536]{2,1,0:T(8,128)(2,1)}, bf16[8,48,1536]{2,1,0:T(8,128)(2,1)}, u32[]{:S(2)}, u32[]{:S(2)}) collective-permute-start(bf16[8,48,1536]{2,1,0:T(8,128)(2,1)} %slice.459), channel_id=1, source_target_pairs={{0,2},{1,5},{2,0},{3,7},{4,6},{5,1},{6,4},{7,3},{8,10},{9,13},{10,... | collective-permute-start | bytes 3538952 | tf_op jit(solution)/shard_map/ppermute | solution.py:49
  467.4 39.2 %all-to-all-start.4 = ((bf16[32,16,768]{2,1,0:T(8,128)(2,1)}), bf16[32,16,768]{2,1,0:T(8,128)(2,1)}, u32[]{:S(2)}, u32[]{:S(2)}) async-start(bf16[32,16,768]{2,1,0:T(8,128)(2,1)} %bitcast.42), calls=%async_computation.4 | async-start | bytes 1572864 | tf_op jit(solution)/shard_map/all_to_all | solution.py:181
  474.8 34.0 %collective-permute-start.45 = (bf16[4,96,768]{2,1,0:T(8,128)(2,1)S(1)}, bf16[4,96,768]{2,1,0:T(8,128)(2,1)}, u32[]{:S(2)}, u32[]{:S(2)}) collective-permute-start(bf16[4,96,768]{2,1,0:T(8,128)(2,1)S(1)} %slice.473), channel_id=1, source_target_pairs={{0,4},{1,3},{2,6},{3,1},{4,0},{5,7},{6,2},{7,5},{8,12},{9,11},{10,... | collective-permute-start | bytes 1769480 | tf_op jit(solution)/shard_map/ppermute | solution.py:49
  526.5 17.2 %collective-permute-start.47 = (bf16[1,96,768]{2,1,0:T(8,128)(2,1)S(1)}, bf16[1,96,768]{2,1,0:T(8,128)(2,1)S(1)}, u32[]{:S(2)}, u32[]{:S(2)}) collective-permute-start(bf16[1,96,768]{2,1,0:T(8,128)(2,1)S(1)} %slice.477), channel_id=1, source_target_pairs={{0,24},{1,25},{2,26},{3,27},{4,28},{5,29},{6,30},{7,31},{8,16},{9,... | collective-permute-start | bytes 442376 | tf_op jit(solution)/shard_map/ppermute | solution.py:49
  (77 other events, 828.1 us)
